TPU v7x, 512 devices: a whole 4x8x8 slice. The times are simulated.
512 devices in a mesh: box: 128 (over z, y, core), col: 4 (over x).
Axes of the slice: x: 4, y: 8, z: 8, core: 2. Of those that a mesh axis runs over, the one named last changes fastest.
Arguments:
- basis: float32 [4, 2, 64, 65536], P(None, None, 'col', 'box'), may hold values from -1000 to 1000
- offsets: float32 [3, 65536], P(None, 'box'), may hold values from -0.5 to 0.5
- weights: float32 [65536], P('box'), may hold values from 0.03 to 0.3
- interp: float32 [512, 32, 128], P('box'), may hold values from 0 to 1
- skeleton: int32 [512, 32], P('box'), may hold values from 0 to 127, as said below
- near_boxes: int32 [512, 27], P('box'), may hold values from 0 to 511, as said below
- near_count: int32 [512], P('box'), may hold values from 3 to 27, as said below
Outputs:
- new_block: float32 [2, 64, 65536], P(None, 'col', 'box')
- coupling: float32 [4, 64, 64], replicated
- factor: float32 [64, 64], replicated
Inputs may be any that keep to these rules, and one draw needn't show every extreme that they name: `skeleton`: each row holds 32 different points of the box. `near_boxes`: entry 0 of box b's row is b itself, entry 1 is b + 4 and entry 2 is b - 4, both clipped to the boxes; every entry lies within 4 boxes of b. Box b's near field is the first near_count[b] entries of its row of near_boxes.
All inputs are finite; a program needn't handle non-finite values.
Results may differ from a plain program's by a relative error of at most 0.0003.
Values sent between devices are 32-bit elements; how exact they have to be, the bound alone decides.
No kernel may reach another device: no remote copies, remote signals or barrier semaphores. Data moves between devices by JAX's collectives and lax.ppermute only.
A program may use at most 64 MiB of HBM per device.

v0:
```python
import math
import jax
import jax.numpy as jnp
from jax import lax
from jax.sharding import PartitionSpec as P

BOX_DEV = 4
WAVENUMBER = 6.0
SMOOTHING = 0.1
SHIFT_SCALE = 0.02
EPSILON = 1e-06
HIGHEST = lax.Precision.HIGHEST
SOURCE_BLOCK = 2048


def extended_2(cells, sides, width):
    for axis, dim in sides:
        count = lax.axis_size(axis)
        ends = count - 1
        head = lax.slice_in_dim(cells, 0, width, axis=dim)
        tail = lax.slice_in_dim(cells, cells.shape[dim] - width, cells.shape[dim], axis=dim)
        cells = jnp.concatenate(
            [
                lax.ppermute(tail, axis, [(i, (i + 1) % count) for i in range(ends)]),
                cells,
                lax.ppermute(head, axis, [((i + 1) % count, i) for i in range(ends)]),
            ],
            axis=dim,
        )
    return cells


def box_centers(box_index):
    along_band = (box_index // BOX_DEV).astype(jnp.float32)
    across = (box_index % BOX_DEV).astype(jnp.float32)
    return jnp.stack([along_band, across, jnp.zeros_like(along_band)])


def helmholtz_pair(targets, sources):
    spread = SMOOTHING * SMOOTHING
    for axis_index in range(3):
        spread = (
            spread + (targets[axis_index][..., :, None] - sources[axis_index][..., None, :]) ** 2
        )
    distance = jnp.sqrt(spread)
    factor = 1.0 / (4.0 * math.pi * distance)
    return (jnp.cos(WAVENUMBER * distance) * factor, jnp.sin(WAVENUMBER * distance) * factor)


def far_block(skel_count, target_pos, target_weight, running, shard_piece, first_row):
    value_rows = shard_piece.shape[0] - 3
    source_count = shard_piece.shape[1]
    source_boxes = source_count // skel_count
    target_count = target_pos.shape[1]
    box_weight = lax.dynamic_slice_in_dim(target_weight, first_row // skel_count, source_boxes, 1)
    kernel_re, kernel_im = helmholtz_pair(target_pos, shard_piece[value_rows:])
    kernel_re = (
        kernel_re.reshape(target_count, source_boxes, skel_count) * box_weight[:, :, None]
    ).reshape(target_count, source_count)
    kernel_im = (
        kernel_im.reshape(target_count, source_boxes, skel_count) * box_weight[:, :, None]
    ).reshape(target_count, source_count)
    stacked = jnp.stack([kernel_re, kernel_im])
    charge_rows = shard_piece[:value_rows].reshape(2, value_rows // 2, source_count)
    product = jnp.einsum("gts,pcs->gpct", stacked, charge_rows, precision=HIGHEST)
    return running + jnp.stack([product[0, 0] - product[1, 1], product[1, 0] + product[0, 1]])


def far_fold(skel_count, target_pos, target_weight, running, shard_piece):
    source_count = shard_piece.shape[1]

    def one_block(block_index, carry):
        offset = block_index * SOURCE_BLOCK
        block_piece = lax.dynamic_slice_in_dim(shard_piece, offset, SOURCE_BLOCK, 1)
        return far_block(skel_count, target_pos, target_weight, carry, block_piece, offset)

    return lax.fori_loop(0, source_count // SOURCE_BLOCK, one_block, running)


def shards(basis, offsets, weights, interp, skeleton, near_boxes, near_count):
    box_count = near_count.shape[0]
    points = interp.shape[2]
    skel_count = interp.shape[1]
    slot_count = near_boxes.shape[1]
    prior_blocks = basis.shape[0]
    columns = basis.shape[2]
    total_boxes = box_count * lax.axis_size("box")
    first_box = lax.axis_index("box") * box_count
    own_boxes = first_box + jnp.arange(box_count, dtype=jnp.int32)
    positions = offsets.reshape(3, box_count, points) + box_centers(own_boxes)[:, :, None]
    current = basis[prior_blocks - 1]
    sources = (current * weights).reshape(2, columns, box_count, points)
    payload = jnp.concatenate([sources.reshape(2 * columns, box_count, points), positions], axis=0)
    extended = extended_2(payload, (("box", 1),), box_count)

    def near_slot(slot_index, running):
        listed = lax.dynamic_index_in_dim(near_boxes, slot_index, 1, keepdims=False)
        live_slot = (slot_index < near_count).astype(jnp.float32)
        picked = jnp.take(extended, listed - first_box + box_count, axis=1)
        source_pos = picked[2 * columns :]
        source_val = (picked[: 2 * columns] * live_slot[None, :, None]).reshape(
            2, columns, box_count, points
        )
        kernel_re, kernel_im = helmholtz_pair(positions, source_pos)
        stacked = jnp.stack([kernel_re, kernel_im])
        product = jnp.einsum("gbtq,pcbq->gpcbt", stacked, source_val, precision=HIGHEST)
        return running + jnp.stack([product[0, 0] - product[1, 1], product[1, 0] + product[0, 1]])

    near_init = jnp.zeros((2, columns, box_count, points), jnp.float32)
    near_field = lax.fori_loop(0, slot_count, near_slot, near_init)
    charges = jnp.einsum("bkq,pcbq->pcbk", interp, sources, precision=HIGHEST).reshape(
        2, columns, box_count * skel_count
    )
    skel_pos = jnp.take_along_axis(
        positions, jnp.broadcast_to(skeleton[None], (3, box_count, skel_count)), axis=2
    ).reshape(3, box_count * skel_count)
    slot_live = jnp.arange(slot_count, dtype=jnp.int32)[None, :] < near_count[:, None]
    every_box = jnp.arange(total_boxes, dtype=jnp.int32)
    box_listed = jnp.any(
        (near_boxes[:, :, None] == every_box[None, None, :]) & slot_live[:, :, None], axis=1
    )
    target_weight = jnp.repeat(1.0 - box_listed.astype(jnp.float32), skel_count, axis=0)
    payload_far = jnp.concatenate(
        [charges.reshape(2 * columns, box_count * skel_count), skel_pos], axis=0
    )
    zero_phi = jnp.zeros((2, columns, box_count * skel_count), jnp.float32)
    potentials = far_fold(
        skel_count,
        skel_pos,
        target_weight,
        zero_phi,
        lax.all_gather(payload_far, "box", axis=1, tiled=True),
    )
    potentials = potentials.reshape(2, columns, box_count, skel_count)
    far_field = jnp.einsum("bkq,pcbk->pcbq", interp, potentials, precision=HIGHEST)
    applied = 0.5 * current + (near_field + far_field).reshape(2, columns, box_count * points)
    rows_basis, rows_applied = (
        lax.all_to_all(basis, "col", split_axis=3, concat_axis=2, tiled=True),
        lax.all_to_all(applied[None], "col", split_axis=3, concat_axis=2, tiled=True),
    )
    rows_applied = rows_applied[0]
    all_columns = rows_applied.shape[1]
    row_total = rows_applied.shape[2] * lax.axis_size("box") * lax.axis_size("col")
    part_coupling = (
        jnp.einsum("kpiq,pjq->kij", rows_basis, rows_applied, precision=HIGHEST) / row_total
    )
    coupling = lax.psum(part_coupling, ("box", "col"))
    residual = rows_applied - jnp.einsum("kpiq,kij->pjq", rows_basis, coupling, precision=HIGHEST)
    part_gram = jnp.einsum("piq,pjq->ij", residual, residual, precision=HIGHEST) / row_total
    gram_matrix = lax.psum(part_gram, ("box", "col"))
    identity = jnp.eye(all_columns, dtype=jnp.float32)
    shift_term = SHIFT_SCALE * jnp.trace(gram_matrix) / all_columns + EPSILON
    lower_factor = jnp.linalg.cholesky(gram_matrix + shift_term * identity)
    inverse = jax.scipy.linalg.solve_triangular(lower_factor, identity, lower=True)
    normalized = jnp.einsum("ij,pjq->piq", inverse, residual, precision=HIGHEST)
    new_block = lax.all_to_all(normalized, "col", split_axis=1, concat_axis=2, tiled=True)
    return (new_block, coupling, lower_factor.T)


def solution(mesh):
    return jax.shard_map(
        shards,
        mesh=mesh,
        in_specs=(
            P(None, None, "col", "box"),
            P(None, "box"),
            P("box"),
            P("box", None, None),
            P("box", None),
            P("box", None),
            P("box"),
        ),
        out_specs=(P(None, "col", "box"), P(), P()),
        check_vma=False,
    )
```

profile of v0, /device:TPU:8, one launch (start us, length us, event | category | flops | bytes accessed | tf_op | source)
XLA Modules:
  0.0 589.9 jit_solution(7123391067058255241)
XLA Ops:
  9.8 1.9 collective-permute-start
  11.7 3.6 collective-permute-start.1
  18.5 3.8 gather_fusion.1
  24.4 2.3 reshape.851
  26.7 4.3 all-to-all-start.1
  31.5 71.1 %while.32 = (s32[]{:T(128)}, f32[2,16,4,128]{3,1,2,0:T(8,128)S(1)}, s32[4,27]{0,1:T(8,128)S(1)}, s32[]{:T(128)}, f32[35,12,128]{2,0,1:T(8,128)S(1)}, /*index=5*/...) while((s32[]{:T(128)}, f32[2,16,4,128]{3,1,2,0:T(8,128)S(1)}, ...), condition=%wide.region_1.2_spmd.clone, body=%wide.region_0.1_spmd.clone.sunk | while | flops 51481128 | bytes 2097387 | solution.py:110
  102.6 8.3 %all-gather.2.cloned.1.call-done = f32[35,16384]{1,0:T(8,128)} async-done(((f32[35,128]{1,0:T(8,128)}), f32[35,16384]{1,0:T(8,128)}) %all-gather.2.cloned.1.call-update) | async-done | bytes 2293776 | tf_op jit(solution)/shard_map/all_gather | solution.py:132
  110.9 73.7 %while.33 = (s32[]{:T(128)}, f32[2,16,128]{2,1,0:T(8,128)S(1)}, f32[35,16384]{1,0:T(8,128)}, f32[3,128]{1,0:T(4,128)S(1)}, f32[128,512]{0,1:T(8,128)S(1)}, /*ind...) while((s32[]{:T(128)}, f32[2,16,128]{2,1,0:T(8,128)S(1)}, ...), condition=%wide.region_4.5_spmd.clone, body=%wide.region_3.4_spmd.clone.sunk | while | flops 206061600 | bytes 9483192 | solution.py:77
  112.5 4.7 multiply_multiply_fusion.3
  118.1 1.9 fusion.58
  121.7 4.7 multiply_multiply_fusion.3
  127.3 1.9 fusion.58
  130.9 4.7 multiply_multiply_fusion.3
  136.6 1.9 fusion.58
  140.1 4.7 multiply_multiply_fusion.3
  145.8 1.9 fusion.58
  149.3 4.7 multiply_multiply_fusion.3
  155.0 1.9 fusion.58
  158.6 4.7 multiply_multiply_fusion.3
  164.2 1.9 fusion.58
  167.8 4.7 multiply_multiply_fusion.3
  173.5 1.9 fusion.58
  177.0 4.7 multiply_multiply_fusion.3
  182.7 1.9 fusion.58
  186.7 4.1 all-to-all-start
  200.3 262.5 %all-reduce.2.cloned.1.call-done = f32[4,64,64]{1,2,0:T(8,128)} async-done(((f32[4,64,64]{1,2,0:T(8,128)}), f32[4,64,64]{1,2,0:T(8,128)}) %all-reduce.2.cloned.1.call-update) | async-done | bytes 65552 | tf_op jit(solution)/shard_map/psum | solution.py:147
  464.3 94.6 %psum.15 = f32[64,64]{1,0:T(8,128)S(1)} all-reduce(f32[64,64]{1,0:T(8,128)S(1)} %fusion.18), channel_id=1, replica_groups=mesh['box'=128,'col'=4] {'box','col'}, use_global_device_ids=true, to_apply=%region_6.7 | all-reduce | flops 4096 | bytes 32768 | tf_op jit(solution)/shard_map/psum | solution.py:150
  560.3 5.8 cholesky.18
  567.5 4.9 custom-call.7
  573.5 3.3 all-to-all-start.2
  577.5 1.7 copy.143
  579.1 3.2 all-to-all-done.2
  (505 shorter events, 113.9 us)
Async XLA Ops:
  7.2 15.1 %copy-start = (f32[4,32,128]{2,1,0:T(8,128)S(1)}, f32[4,32,128]{2,1,0:T(8,128)}, u32[]{:S(2)}) copy-start(f32[4,32,128]{2,1,0:T(8,128)} %param.14) | copy-start | bytes 196612
  7.2 103.8 %all-gather.2.cloned.1.call-start = ((), (), s32[]{:S(2)}) async-start(), calls=%async_computation.3 | async-start | bytes 2641920 | tf_op jit(solution)/shard_map/all_gather | solution.py:132
  9.8 21.7 %collective-permute-start = (f32[35,4,128]{2,0,1:T(8,128)S(1)}, f32[35,4,128]{2,0,1:T(8,128)S(1)}, u32[]{:S(2)}, u32[]{:S(2)}) collective-permute-start(f32[35,4,128]{2,0,1:T(8,128)S(1)} %pad_maximum_fusion.1), channel_id=1, source_target_pairs={{0,4},{4,8},{8,12},{12,16},{16,20},{20,24},{24,28},{28,32},{32,36}... | collective-permute-start | bytes 215048 | tf_op jit(solution)/shard_map/ppermute | solution.py:24
  11.7 19.8 %collective-permute-start.1 = (f32[35,4,128]{2,0,1:T(8,128)S(1)}, f32[35,4,128]{2,0,1:T(8,128)S(1)}, u32[]{:S(2)}, u32[]{:S(2)}) collective-permute-start(f32[35,4,128]{2,0,1:T(8,128)S(1)} %pad_maximum_fusion.1), channel_id=1, source_target_pairs={{4,0},{8,4},{12,8},{16,12},{20,16},{24,20},{28,24},{32,28},{36,32}... | collective-permute-start | bytes 215048 | tf_op jit(solution)/shard_map/ppermute | solution.py:26
  18.5 3.9 copy-start.2
  18.5 4.9 copy-start.1
  23.4 7.7 %copy-start.3 = (s32[4,27]{1,0:T(4,128)S(1)}, s32[4,27]{1,0:T(4,128)}, u32[]{:S(2)}) copy-start(s32[4,27]{1,0:T(4,128)} %param.16) | copy-start | bytes 1300
  23.4 7.7 %copy-start.4 = (s32[4]{0:T(128)S(1)}, s32[4]{0:T(128)}, u32[]{:S(2)}) copy-start(s32[4]{0:T(128)} %param.17) | copy-start | bytes 52
  26.7 160.0 %all-to-all-start.1 = ((f32[4,1,16384]{2,1,0:T(1,128)}), f32[4,1,16384]{2,1,0:T(1,128)S(1)}, u32[]{:S(2)}, u32[]{:S(2)}) async-start(f32[4,1,16384]{2,1,0:T(1,128)} %reshape.851), calls=%async_computation.1 | async-start | bytes 524288 | tf_op jit(solution)/shard_map/all_to_all | solution.py:138
  186.7 9.8 %all-to-all-start = ((f32[4,1,4096]{2,1,0:T(1,128)}), f32[4,1,4096]{2,1,0:T(1,128)S(1)}, u32[]{:S(2)}, u32[]{:S(2)}) async-start(f32[4,1,4096]{2,1,0:T(1,128)} %reshape.849), calls=%async_computation | async-start | bytes 131072 | tf_op jit(solution)/shard_map/all_to_all | solution.py:139
  190.8 272.0 %all-reduce.2.cloned.1.call-start = ((), (), s32[]{:S(2)}) async-start(), calls=%async_computation.4 | async-start | bytes 262144 | tf_op jit(solution)/shard_map/psum | solution.py:147
  573.5 8.9 %all-to-all-start.2 = ((f32[2,64,128]{2,0,1:T(2,128)}), f32[2,64,128]{2,0,1:T(2,128)S(1)}, u32[]{:S(2)}, u32[]{:S(2)}) async-start(f32[2,64,128]{2,0,1:T(2,128)} %copy.141), calls=%async_computation.2 | async-start | bytes 131072 | tf_op jit(solution)/shard_map/all_to_all | solution.py:156
Sparse Core Ops, SparseCore 0:
  23.5 87.4 all-gather.1
  199.5 263.3 all-reduce.1
where the time goes:
time: 591 us; the launch traced here: 590 us
  waiting for transfers between devices  275 us (47%)
  blocking collectives  94.6 us (16%)
  other arithmetic  93.7 us (16%)
  local copies, waits for them, and re-layouts  55.6 us (9%)
  matrix products  34.8 us (6%)
  starting transfers between devices  17.3 us (3%)
  between operations  15.1 us (3%)
    psum x1, waiting for transfers between devices, shards(): coupling = lax.psum(part_coupling, ('box', 'col'))  263 us
    psum x1, blocking collectives, shards(): gram_matrix = lax.psum(part_gram, ('box', 'col'))  94.6 us
    mul x8, other arithmetic, far_block(): kernel_re.reshape(target_count, source_boxes, skel_count)  37.5 us
    mul x27, other arithmetic, helmholtz_pair(): jnp.cos(WAVENUMBER * distance) * factor  31.7 us
    dot_general x27, matrix products, near_slot(): jnp.einsum('gbtq,pcbq->gpcbt', stacked, source_val, precision=HIGHEST)  15.9 us
    dot_general x8, matrix products, far_block(): jnp.einsum('gts,pcs->gpct', stacked, charge_rows, precision=HIGHEST)  15.4 us
    gather x27, local copies, waits for them, and re-layouts, near_slot(): picked = jnp.take(extended, listed - first_box + box_count, axis=1)  15 us
  transfers between devices with their start and end apart: 7, of which 4 were waited for; matrix products, arithmetic and copies ran while one was open for 28% of the time, Pallas kernels for 0%

commit v1 on v0

--- a/solution.py
+++ b/solution.py
@@ -144,7 +144,8 @@
     part_coupling = (
         jnp.einsum("kpiq,pjq->kij", rows_basis, rows_applied, precision=HIGHEST) / row_total
     )
-    coupling = lax.psum(part_coupling, ("box", "col"))
+    partial = lax.psum(part_coupling, "col")
+    coupling = lax.psum(partial, "box")
     residual = rows_applied - jnp.einsum("kpiq,kij->pjq", rows_basis, coupling, precision=HIGHEST)
     part_gram = jnp.einsum("piq,pjq->ij", residual, residual, precision=HIGHEST) / row_total
     gram_matrix = lax.psum(part_gram, ("box", "col"))

time: 591 us -> 567 us (0.959)
  the two profiles are of different devices: /device:TPU:8 before, /device:TPU:1 now
where the time goes in v1:
time: 567 us; the launch traced here: 566 us
  waiting for transfers between devices  247 us (44%)
  blocking collectives  95.3 us (17%)
  other arithmetic  93.7 us (17%)
  local copies, waits for them, and re-layouts  55.6 us (10%)
  matrix products  34.8 us (6%)
  starting transfers between devices  20.8 us (4%)
  between operations  14.8 us (3%)
    psum x1, waiting for transfers between devices, shards(): coupling = lax.psum(partial, 'box')  190 us
    psum x1, blocking collectives, shards(): gram_matrix = lax.psum(part_gram, ('box', 'col'))  95.3 us
    psum x1, waiting for transfers between devices, shards(): partial = lax.psum(part_coupling, 'col')  48.6 us
    mul x8, other arithmetic, far_block(): kernel_re.reshape(target_count, source_boxes, skel_count)  37.5 us
    mul x27, other arithmetic, helmholtz_pair(): jnp.cos(WAVENUMBER * distance) * factor  31.7 us
    dot_general x27, matrix products, near_slot(): jnp.einsum('gbtq,pcbq->gpcbt', stacked, source_val, precision=HIGHEST)  15.9 us
    dot_general x8, matrix products, far_block(): jnp.einsum('gts,pcs->gpct', stacked, charge_rows, precision=HIGHEST)  15.4 us
    gather x27, local copies, waits for them, and re-layouts, near_slot(): picked = jnp.take(extended, listed - first_box + box_count, axis=1)  15 us
  transfers between devices with their start and end apart: 8, of which 5 were waited for; matrix products, arithmetic and copies ran while one was open for 29% of the time, Pallas kernels for 0%

profile of v1, /device:TPU:1, one launch (start us, length us, event | category | flops | bytes accessed | tf_op | source)
XLA Modules:
  0.0 565.5 jit_solution(9630037974180762965)
XLA Ops:
  9.8 4.6 collective-permute-start
  14.4 5.5 collective-permute-start.1
  22.9 3.8 gather_fusion.1
  28.9 2.3 reshape.851
  31.2 3.4 all-to-all-start.1
  35.1 71.1 %while.32 = (s32[]{:T(128)}, f32[2,16,4,128]{3,1,2,0:T(8,128)S(1)}, s32[4,27]{0,1:T(8,128)S(1)}, s32[]{:T(128)}, f32[35,12,128]{2,0,1:T(8,128)S(1)}, /*index=5*/...) while((s32[]{:T(128)}, f32[2,16,4,128]{3,1,2,0:T(8,128)S(1)}, ...), condition=%wide.region_1.2_spmd.clone, body=%wide.region_0.1_spmd.clone.sunk | while | flops 51481128 | bytes 2097387 | solution.py:110
  106.2 6.0 %all-gather.2.cloned.1.call-done = f32[35,16384]{1,0:T(8,128)} async-done(((f32[35,128]{1,0:T(8,128)}), f32[35,16384]{1,0:T(8,128)}) %all-gather.2.cloned.1.call-update) | async-done | bytes 2293776 | tf_op jit(solution)/shard_map/all_gather | solution.py:132
  112.3 73.7 %while.33 = (s32[]{:T(128)}, f32[2,16,128]{2,1,0:T(8,128)S(1)}, f32[35,16384]{1,0:T(8,128)}, f32[3,128]{1,0:T(4,128)S(1)}, f32[128,512]{0,1:T(8,128)S(1)}, /*ind...) while((s32[]{:T(128)}, f32[2,16,128]{2,1,0:T(8,128)S(1)}, ...), condition=%wide.region_4.5_spmd.clone, body=%wide.region_3.4_spmd.clone.sunk | while | flops 206061600 | bytes 9483192 | solution.py:77
  113.8 4.7 multiply_multiply_fusion.3
  119.5 1.9 fusion.58
  123.0 4.7 multiply_multiply_fusion.3
  128.7 1.9 fusion.58
  132.2 4.7 multiply_multiply_fusion.3
  137.9 1.9 fusion.58
  141.5 4.7 multiply_multiply_fusion.3
  147.1 1.9 fusion.58
  150.7 4.7 multiply_multiply_fusion.3
  156.4 1.9 fusion.58
  159.9 4.7 multiply_multiply_fusion.3
  165.6 1.9 fusion.58
  169.1 4.7 multiply_multiply_fusion.3
  174.8 1.9 fusion.58
  178.3 4.7 multiply_multiply_fusion.3
  184.0 1.9 fusion.58
  188.0 3.9 all-to-all-start
  199.4 48.6 %all-reduce.3.cloned.1.call-done = f32[4,64,64]{1,2,0:T(8,128)} async-done(((f32[4,64,64]{1,2,0:T(8,128)}), f32[4,64,64]{1,2,0:T(8,128)}) %all-reduce.3.cloned.1.call-update) | async-done | bytes 65552 | tf_op jit(solution)/shard_map/psum | solution.py:147
  249.0 190.3 %all-reduce.5.cloned.1.call-done = f32[4,64,64]{1,2,0:T(8,128)} async-done(((f32[4,64,64]{1,2,0:T(8,128)}), f32[4,64,64]{1,2,0:T(8,128)}) %all-reduce.5.cloned.1.call-update) | async-done | bytes 65552 | tf_op jit(solution)/shard_map/psum | solution.py:148
  440.7 95.3 %psum.23 = f32[64,64]{1,0:T(8,128)S(1)} all-reduce(f32[64,64]{1,0:T(8,128)S(1)} %fusion.18), channel_id=1, replica_groups=mesh['box'=128,'col'=4] {'box','col'}, use_global_device_ids=true, to_apply=%region_7.8 | all-reduce | flops 4096 | bytes 32768 | tf_op jit(solution)/shard_map/psum | solution.py:151
  537.4 5.8 %cholesky.18 = f32[64,64]{1,0:T(8,128)S(1)} custom-call(f32[64,64]{1,0:T(8,128)S(1)} %fusion.26), custom_call_target="Cholesky" | custom-call | tf_op jit(solution)/shard_map/jit(cholesky)/cholesky | solution.py:154
  544.6 4.9 custom-call.7
  550.6 3.3 all-to-all-start.2
  556.2 2.1 all-to-all-done.2
  (508 shorter events, 114.5 us)
Async XLA Ops:
  7.2 19.6 %copy-start = (f32[4,32,128]{2,1,0:T(8,128)S(1)}, f32[4,32,128]{2,1,0:T(8,128)}, u32[]{:S(2)}) copy-start(f32[4,32,128]{2,1,0:T(8,128)} %param.14) | copy-start | bytes 196612
  7.2 105.1 %all-gather.2.cloned.1.call-start = ((), (), s32[]{:S(2)}) async-start(), calls=%async_computation.3 | async-start | bytes 2641920 | tf_op jit(solution)/shard_map/all_gather | solution.py:132
  9.8 25.3 %collective-permute-start = (f32[35,4,128]{2,0,1:T(8,128)S(1)}, f32[35,4,128]{2,0,1:T(8,128)S(1)}, u32[]{:S(2)}, u32[]{:S(2)}) collective-permute-start(f32[35,4,128]{2,0,1:T(8,128)S(1)} %pad_maximum_fusion.1), channel_id=1, source_target_pairs={{0,4},{4,8},{8,12},{12,16},{16,20},{20,24},{24,28},{28,32},{32,36}... | collective-permute-start | bytes 215048 | tf_op jit(solution)/shard_map/ppermute | solution.py:24
  14.4 20.7 %collective-permute-start.1 = (f32[35,4,128]{2,0,1:T(8,128)S(1)}, f32[35,4,128]{2,0,1:T(8,128)S(1)}, u32[]{:S(2)}, u32[]{:S(2)}) collective-permute-start(f32[35,4,128]{2,0,1:T(8,128)S(1)} %pad_maximum_fusion.1), channel_id=1, source_target_pairs={{4,0},{8,4},{12,8},{16,12},{20,16},{24,20},{28,24},{32,28},{36,32}... | collective-permute-start | bytes 215048 | tf_op jit(solution)/shard_map/ppermute | solution.py:26
  22.9 3.9 copy-start.2
  22.9 4.9 copy-start.1
  27.8 6.8 %copy-start.3 = (s32[4,27]{1,0:T(4,128)S(1)}, s32[4,27]{1,0:T(4,128)}, u32[]{:S(2)}) copy-start(s32[4,27]{1,0:T(4,128)} %param.16) | copy-start | bytes 1300
  27.8 6.9 %copy-start.4 = (s32[4]{0:T(128)S(1)}, s32[4]{0:T(128)}, u32[]{:S(2)}) copy-start(s32[4]{0:T(128)} %param.17) | copy-start | bytes 52
  31.2 156.8 %all-to-all-start.1 = ((f32[4,1,16384]{2,1,0:T(1,128)}), f32[4,1,16384]{2,1,0:T(1,128)S(1)}, u32[]{:S(2)}, u32[]{:S(2)}) async-start(f32[4,1,16384]{2,1,0:T(1,128)} %reshape.851), calls=%async_computation.1 | async-start | bytes 524288 | tf_op jit(solution)/shard_map/all_to_all | solution.py:138
  188.0 8.4 %all-to-all-start = ((f32[4,1,4096]{2,1,0:T(1,128)}), f32[4,1,4096]{2,1,0:T(1,128)S(1)}, u32[]{:S(2)}, u32[]{:S(2)}) async-start(f32[4,1,4096]{2,1,0:T(1,128)} %reshape.849), calls=%async_computation | async-start | bytes 131072 | tf_op jit(solution)/shard_map/all_to_all | solution.py:139
  192.0 56.0 %all-reduce.3.cloned.1.call-start = ((), (), s32[]{:S(2)}) async-start(), calls=%async_computation.4 | async-start | bytes 262144 | tf_op jit(solution)/shard_map/psum | solution.py:147
  199.3 239.9 %all-reduce.5.cloned.1.call-start = ((), (), s32[]{:S(2)}) async-start(), calls=%async_computation.5 | async-start | bytes 262144 | tf_op jit(solution)/shard_map/psum | solution.py:148
  550.6 7.7 %all-to-all-start.2 = ((f32[2,64,128]{2,0,1:T(2,128)}), f32[2,64,128]{2,0,1:T(2,128)S(1)}, u32[]{:S(2)}, u32[]{:S(2)}) async-start(f32[2,64,128]{2,0,1:T(2,128)} %copy.141), calls=%async_computation.2 | async-start | bytes 131072 | tf_op jit(solution)/shard_map/all_to_all | solution.py:157
Sparse Core Ops, SparseCore 0:
  27.9 84.2 all-gather.1
  199.5 48.4 all-reduce.2
  251.2 188.0 all-reduce.4
